TPU v7x, 32 devices: a whole 2x2x4 slice. The times are simulated.
32 devices in a mesh: sample: 4 (over x, core), space: 8 (over z, y).
Axes of the slice: x: 2, y: 2, z: 4, core: 2. Of those that a mesh axis runs over, the one named last changes fastest.
Arguments:
- activations: bfloat16 [4, 64, 32, 1024], P('sample', 'space'), may hold values from -6 to 6
- open_cells: int32 [4, 64, 512], P('sample', 'space'), may hold values 0 or 1
- wind_class: int32 [4], P('sample'), may hold values from 0 to 7
- w_early: bfloat16 [3, 3, 3, 64, 128], replicated, may hold values from -0.15625 to 0.15625
- bias_table: float32 [8, 128], replicated, may hold values from -3 to 3
- w_deep: bfloat16 [2, 2, 2, 128, 256], replicated, may hold values from -0.1875 to 0.1875
- cotangent: bfloat16 [4, 16, 8, 1024], P('sample', 'space'), may hold values from -0.119628906 to 0.119628906
Outputs:
- deep: bfloat16 [4, 16, 8, 1024], P('sample', 'space')
- grad_deep: float32 [2, 2, 2, 128, 256], replicated
- grad_early: float32 [3, 3, 3, 64, 128], replicated
All inputs are finite; a program needn't handle non-finite values. No bound on the sum of `open_cells` on one device may be relied on, other than what follows from the above.
Results may differ from a plain program's by a relative error of at most 0.005.
Values may be sent and summed in bfloat16 or wider, within the bound.
No kernel may reach another device: no remote copies, remote signals or barrier semaphores. Data moves between devices by JAX's collectives and lax.ppermute only.
A program may use at most 64 MiB of HBM per device.

v0:
```python
import jax
import jax.numpy as jnp
from jax import lax
from jax.sharding import PartitionSpec as P

SLOPE = 0.3


def passed_along(value, axis, by):
    peers = lax.axis_size(axis)
    pairs = [(i, i + by) for i in range(peers) if 0 <= i + by < peers]
    return lax.ppermute(value, axis, pairs)


def early_forward(padded, w_early, bias):
    out = lax.conv_general_dilated(
        padded[None],
        w_early,
        (2, 2, 2),
        ((0, 0), (0, 0), (0, 0)),
        dimension_numbers=("NDHWC", "DHWIO", "NDHWC"),
        preferred_element_type=jnp.float32,
    )
    return out[0] + bias


def deep_terms(hidden, w_deep, upstream):
    zh, yh, xh, c1 = hidden.shape
    c2 = w_deep.shape[4]
    patches = (
        hidden.reshape(zh // 2, 2, yh // 2, 2, xh // 2, 2, c1)
        .transpose(0, 2, 4, 1, 3, 5, 6)
        .reshape(-1, 8 * c1)
    )
    out = jnp.dot(patches, w_deep.reshape(8 * c1, c2), preferred_element_type=jnp.float32)
    flat_up = upstream.reshape(-1, c2)
    grad_w = lax.dot_general(
        patches, flat_up, (((0,), (0,)), ((), ())), preferred_element_type=jnp.float32
    ).reshape(2, 2, 2, c1, c2)
    back = lax.dot_general(
        flat_up,
        w_deep.reshape(8, c1, c2),
        (((1,), (2,)), ((), ())),
        preferred_element_type=jnp.float32,
    )
    back = (
        back.reshape(zh // 2, yh // 2, xh // 2, 2, 2, 2, c1)
        .transpose(0, 3, 1, 4, 2, 5, 6)
        .reshape(zh, yh, xh, c1)
    )
    return (out, grad_w, back)


def early_grad(padded, delta):
    zo, yo, xo, c1 = delta.shape
    c0 = padded.shape[3]
    flat_delta = delta.reshape(-1, c1)
    pieces = []
    for a in range(3):
        for b in range(3):
            for c in range(3):
                piece = lax.slice(
                    padded,
                    (a, b, c, 0),
                    (a + 2 * zo - 1, b + 2 * yo - 1, c + 2 * xo - 1, c0),
                    (2, 2, 2, 1),
                ).reshape(-1, c0)
                pieces.append(
                    lax.dot_general(
                        piece,
                        flat_delta,
                        (((0,), (0,)), ((), ())),
                        preferred_element_type=jnp.float32,
                    )
                )
    return jnp.stack(pieces).reshape(3, 3, 3, c0, c1)


def total_terms(grad):
    flat = grad.reshape(-1)
    summed = lax.psum(flat, ("sample", "space"))
    return summed.reshape(grad.shape)


def body(activations, open_cells, wind_class, w_early, bias_table, w_deep, cotangent):
    depth = activations.shape[1]
    rows_y = activations.shape[2]
    chan_in = w_early.shape[3]
    chan_out = w_deep.shape[4]
    rows_x = activations.shape[3] // chan_in
    opens = open_cells[0].reshape(depth, rows_y, rows_x, 1).astype(jnp.bfloat16)
    masked = (activations[0].reshape(depth, rows_y, rows_x, chan_in) * opens).reshape(
        depth, rows_y, rows_x * chan_in
    )
    below = passed_along(masked[depth - 1], "space", 1)
    field = jnp.concatenate([below[None], masked], axis=0).reshape(
        depth + 1, rows_y, rows_x, chan_in
    )
    padded = jnp.pad(field, ((0, 0), (1, 0), (1, 0), (0, 0)))
    chosen = jnp.arange(bias_table.shape[0], dtype=jnp.int32)[:, None] == wind_class[0]
    bias = jnp.sum(jnp.where(chosen, bias_table, jnp.zeros_like(bias_table)), axis=0)
    pre = early_forward(padded, w_early, bias)
    hidden = jnp.where(pre > 0, pre, SLOPE * pre).astype(jnp.bfloat16)
    upstream = cotangent[0].reshape(depth // 4, rows_y // 4, rows_x // 4, chan_out)
    out, grad_w, back = deep_terms(hidden, w_deep, upstream)
    delta = (back * jnp.where(pre > 0, 1.0, SLOPE)).astype(jnp.bfloat16)
    grad_deep = total_terms(grad_w)
    grad_early = total_terms(early_grad(padded, delta))
    deep = out.astype(jnp.bfloat16).reshape(1, depth // 4, rows_y // 4, rows_x // 4 * chan_out)
    return (deep, grad_deep, grad_early)


def solution(mesh):
    in_specs = (
        P("sample", "space", None, None),
        P("sample", "space", None),
        P("sample"),
        P(),
        P(),
        P(),
        P("sample", "space", None, None),
    )
    out_specs = (P("sample", "space", None, None), P(), P())
    return jax.shard_map(body, mesh=mesh, in_specs=in_specs, out_specs=out_specs, check_vma=False)
```

profile of v0, /device:TPU:0, one launch (start us, length us, event | category | flops | bytes accessed | tf_op | source)
XLA Modules:
  0.0 380.3 jit_solution(18190275280594896844)
XLA Ops:
  7.2 1.8 reshape_squeeze.4
  10.9 4.9 %collective-permute-start = (bf16[32,1024]{1,0:T(8,128)(2,1)S(1)}, bf16[32,1024]{1,0:T(8,128)(2,1)S(1)}, u32[]{:S(2)}, u32[]{:S(2)}) collective-permute-start(bf16[32,1024]{1,0:T(8,128)(2,1)S(1)} %squeeze.11), channel_id=1, source_target_pairs={{0,1},{1,2},{2,3},{3,4},{4,5},{5,6},{6,7},{8,9},{9,10},{10,11},{11... | collective-permute-start | bytes 196616 | tf_op jit(solution)/shard_map/ppermute | solution.py:12
  17.9 1.8 fusion.111
  20.3 9.8 %slice.86 = bf16[4,16,8,64]{3,1,2,0:T(8,128)(2,1)} slice(bf16[9,33,17,64]{3,1,2,0:T(8,128)(2,1)S(1)} %fusion.11), slice={[0:7:2], [0:31:2], [0:15:2], [0:64:1]} | slice | bytes 131072 | tf_op jit(solution)/shard_map/slice | solution.py:62
  30.0 9.7 %slice.87 = bf16[4,16,8,64]{3,1,2,0:T(8,128)(2,1)} slice(bf16[9,33,17,64]{3,1,2,0:T(8,128)(2,1)S(1)} %fusion.11), slice={[0:7:2], [0:31:2], [1:16:2], [0:64:1]} | slice | bytes 131072 | tf_op jit(solution)/shard_map/slice | solution.py:62
  39.8 9.8 %slice.88 = bf16[4,16,8,64]{3,1,2,0:T(8,128)(2,1)} slice(bf16[9,33,17,64]{3,1,2,0:T(8,128)(2,1)S(1)} %fusion.11), slice={[0:7:2], [0:31:2], [2:17:2], [0:64:1]} | slice | bytes 131072 | tf_op jit(solution)/shard_map/slice | solution.py:62
  49.6 9.7 %slice.89 = bf16[4,16,8,64]{3,1,2,0:T(8,128)(2,1)} slice(bf16[9,33,17,64]{3,1,2,0:T(8,128)(2,1)S(1)} %fusion.11), slice={[0:7:2], [1:32:2], [0:15:2], [0:64:1]} | slice | bytes 131072 | tf_op jit(solution)/shard_map/slice | solution.py:62
  59.3 9.7 %slice.90 = bf16[4,16,8,64]{3,1,2,0:T(8,128)(2,1)} slice(bf16[9,33,17,64]{3,1,2,0:T(8,128)(2,1)S(1)} %fusion.11), slice={[0:7:2], [1:32:2], [1:16:2], [0:64:1]} | slice | bytes 131072 | tf_op jit(solution)/shard_map/slice | solution.py:62
  69.0 9.8 %slice.91 = bf16[4,16,8,64]{3,1,2,0:T(8,128)(2,1)} slice(bf16[9,33,17,64]{3,1,2,0:T(8,128)(2,1)S(1)} %fusion.11), slice={[0:7:2], [1:32:2], [2:17:2], [0:64:1]} | slice | bytes 131072 | tf_op jit(solution)/shard_map/slice | solution.py:62
  78.7 9.8 %slice.92 = bf16[4,16,8,64]{3,1,2,0:T(8,128)(2,1)} slice(bf16[9,33,17,64]{3,1,2,0:T(8,128)(2,1)S(1)} %fusion.11), slice={[0:7:2], [2:33:2], [0:15:2], [0:64:1]} | slice | bytes 131072 | tf_op jit(solution)/shard_map/slice | solution.py:62
  88.5 9.7 %slice.93 = bf16[4,16,8,64]{3,1,2,0:T(8,128)(2,1)} slice(bf16[9,33,17,64]{3,1,2,0:T(8,128)(2,1)S(1)} %fusion.11), slice={[0:7:2], [2:33:2], [1:16:2], [0:64:1]} | slice | bytes 131072 | tf_op jit(solution)/shard_map/slice | solution.py:62
  98.2 9.8 %slice.94 = bf16[4,16,8,64]{3,1,2,0:T(8,128)(2,1)} slice(bf16[9,33,17,64]{3,1,2,0:T(8,128)(2,1)S(1)} %fusion.11), slice={[0:7:2], [2:33:2], [2:17:2], [0:64:1]} | slice | bytes 131072 | tf_op jit(solution)/shard_map/slice | solution.py:62
  108.0 9.7 %slice.95 = bf16[4,16,8,64]{3,1,2,0:T(8,128)(2,1)} slice(bf16[9,33,17,64]{3,1,2,0:T(8,128)(2,1)S(1)} %fusion.11), slice={[1:8:2], [0:31:2], [0:15:2], [0:64:1]} | slice | bytes 131072 | tf_op jit(solution)/shard_map/slice | solution.py:62
  117.7 9.7 %slice.96 = bf16[4,16,8,64]{3,1,2,0:T(8,128)(2,1)} slice(bf16[9,33,17,64]{3,1,2,0:T(8,128)(2,1)S(1)} %fusion.11), slice={[1:8:2], [0:31:2], [1:16:2], [0:64:1]} | slice | bytes 131072 | tf_op jit(solution)/shard_map/slice | solution.py:62
  127.4 9.8 %slice.97 = bf16[4,16,8,64]{3,1,2,0:T(8,128)(2,1)} slice(bf16[9,33,17,64]{3,1,2,0:T(8,128)(2,1)S(1)} %fusion.11), slice={[1:8:2], [0:31:2], [2:17:2], [0:64:1]} | slice | bytes 131072 | tf_op jit(solution)/shard_map/slice | solution.py:62
  137.2 9.7 %slice.98 = bf16[4,16,8,64]{3,1,2,0:T(8,128)(2,1)} slice(bf16[9,33,17,64]{3,1,2,0:T(8,128)(2,1)S(1)} %fusion.11), slice={[1:8:2], [1:32:2], [0:15:2], [0:64:1]} | slice | bytes 131072 | tf_op jit(solution)/shard_map/slice | solution.py:62
  146.9 9.7 %slice.99 = bf16[4,16,8,64]{3,1,2,0:T(8,128)(2,1)} slice(bf16[9,33,17,64]{3,1,2,0:T(8,128)(2,1)S(1)} %fusion.11), slice={[1:8:2], [1:32:2], [1:16:2], [0:64:1]} | slice | bytes 131072 | tf_op jit(solution)/shard_map/slice | solution.py:62
  156.6 9.8 %slice.100 = bf16[4,16,8,64]{3,1,2,0:T(8,128)(2,1)} slice(bf16[9,33,17,64]{3,1,2,0:T(8,128)(2,1)S(1)} %fusion.11), slice={[1:8:2], [1:32:2], [2:17:2], [0:64:1]} | slice | bytes 131072 | tf_op jit(solution)/shard_map/slice | solution.py:62
  166.4 9.8 %slice.101 = bf16[4,16,8,64]{3,1,2,0:T(8,128)(2,1)} slice(bf16[9,33,17,64]{3,1,2,0:T(8,128)(2,1)S(1)} %fusion.11), slice={[1:8:2], [2:33:2], [0:15:2], [0:64:1]} | slice | bytes 131072 | tf_op jit(solution)/shard_map/slice | solution.py:62
  176.2 9.7 %slice.102 = bf16[4,16,8,64]{3,1,2,0:T(8,128)(2,1)} slice(bf16[9,33,17,64]{3,1,2,0:T(8,128)(2,1)S(1)} %fusion.11), slice={[1:8:2], [2:33:2], [1:16:2], [0:64:1]} | slice | bytes 131072 | tf_op jit(solution)/shard_map/slice | solution.py:62
  185.9 9.8 %slice.103 = bf16[4,16,8,64]{3,1,2,0:T(8,128)(2,1)} slice(bf16[9,33,17,64]{3,1,2,0:T(8,128)(2,1)S(1)} %fusion.11), slice={[1:8:2], [2:33:2], [2:17:2], [0:64:1]} | slice | bytes 131072 | tf_op jit(solution)/shard_map/slice | solution.py:62
  195.7 9.7 %slice.104 = bf16[4,16,8,64]{3,1,2,0:T(8,128)(2,1)} slice(bf16[9,33,17,64]{3,1,2,0:T(8,128)(2,1)S(1)} %fusion.11), slice={[2:9:2], [0:31:2], [0:15:2], [0:64:1]} | slice | bytes 131072 | tf_op jit(solution)/shard_map/slice | solution.py:62
  235.6 134.6 %all-reduce.4.cloned.1.call-done = (f32[2,2,2,128,256]{4,3,2,1,0:T(8,128)}, f32[3,3,3,64,128]{4,3,2,1,0:T(8,128)}) async-done(((f32[2,2,2,128,256]{4,3,2,1,0:T(8,128)}, f32[3,3,3,64,128]{4,3,2,1,0:T(8,128)}), (f32[2,2,2,128,256]{4,3,2,1,0:T(8,128)}, f32[3,3,3,64,128]{4,3,2,1,0:T(8,128)})) %all-reduce.4.cloned.1.call-update) | async-done | bytes 1933328 | tf_op jit(solution)/shard_map/psum | solution.py:81
  370.2 2.3 copy.90
  (111 shorter events, 34.5 us)
Async XLA Ops:
  7.2 9.4 %copy-start = (bf16[2,2,2,128,256]{4,3,2,1,0:T(8,128)(2,1)S(1)}, bf16[2,2,2,128,256]{4,3,2,1,0:T(8,128)(2,1)}, u32[]{:S(2)}) copy-start(bf16[2,2,2,128,256]{4,3,2,1,0:T(8,128)(2,1)} %param.12) | copy-start | bytes 1572868
  7.2 9.3 %copy-start.3 = (bf16[1,2,8,1024]{3,2,1,0:T(8,128)(2,1)S(1)}, bf16[1,2,8,1024]{3,2,1,0:T(8,128)(2,1)}, u32[]{:S(2)}) copy-start(bf16[1,2,8,1024]{3,2,1,0:T(8,128)(2,1)} %param.13) | copy-start | bytes 98308
  7.2 363.0 %all-reduce.4.cloned.1.call-start = ((), (), s32[]{:S(2)}) async-start(), calls=%async_computation | async-start | bytes 3866624 | tf_op jit(solution)/shard_map/psum | solution.py:81
  9.0 7.9 %copy-start.19 = (f32[8,128]{1,0:T(8,128)S(1)}, f32[8,128]{1,0:T(8,128)}, u32[]{:S(2)}) copy-start(f32[8,128]{1,0:T(8,128)} %param.11) | copy-start | bytes 12292
  10.9 6.8 %collective-permute-start = (bf16[32,1024]{1,0:T(8,128)(2,1)S(1)}, bf16[32,1024]{1,0:T(8,128)(2,1)S(1)}, u32[]{:S(2)}, u32[]{:S(2)}) collective-permute-start(bf16[32,1024]{1,0:T(8,128)(2,1)S(1)} %squeeze.11), channel_id=1, source_target_pairs={{0,1},{1,2},{2,3},{3,4},{4,5},{5,6},{6,7},{8,9},{9,10},{10,11},{11... | collective-permute-start | bytes 196616 | tf_op jit(solution)/shard_map/ppermute | solution.py:12
  216.2 1.0 copy-start.20
  216.2 1.0 copy-start.21
  218.6 3.7 copy-start.16
  218.6 4.9 %copy-start.15 = (bf16[4,16,8,64]{3,1,2,0:T(8,128)(2,1)S(1)}, bf16[4,16,8,64]{3,1,2,0:T(8,128)(2,1)}, u32[]{:S(2)}) copy-start(bf16[4,16,8,64]{3,1,2,0:T(8,128)(2,1)} %slice.89) | copy-start | bytes 196612
  218.6 6.0 %copy-start.14 = (bf16[4,16,8,64]{3,1,2,0:T(8,128)(2,1)S(1)}, bf16[4,16,8,64]{3,1,2,0:T(8,128)(2,1)}, u32[]{:S(2)}) copy-start(bf16[4,16,8,64]{3,1,2,0:T(8,128)(2,1)} %slice.90) | copy-start | bytes 196612
  218.6 6.2 %copy-start.13 = (bf16[4,16,8,64]{3,1,2,0:T(8,128)(2,1)S(1)}, bf16[4,16,8,64]{3,1,2,0:T(8,128)(2,1)}, u32[]{:S(2)}) copy-start(bf16[4,16,8,64]{3,1,2,0:T(8,128)(2,1)} %slice.91) | copy-start | bytes 196612
  219.5 5.1 %copy-start.17 = (bf16[4,16,8,128]{3,1,2,0:T(8,128)(2,1)S(1)}, bf16[4,16,8,128]{3,1,2,0:T(8,128)(2,1)}, u32[]{:S(2)}) copy-start(bf16[4,16,8,128]{3,1,2,0:T(8,128)(2,1)} %fusion.45) | copy-start | bytes 393220
  219.8 7.6 %copy-start.18 = (bf16[4,16,8,128]{3,1,2,0:T(8,128)(2,1)S(1)}, bf16[4,16,8,128]{3,1,2,0:T(8,128)(2,1)}, u32[]{:S(2)}) copy-start(bf16[4,16,8,128]{3,1,2,0:T(8,128)(2,1)} %fusion.45) | copy-start | bytes 393220
  219.8 9.8 %copy-start.12 = (bf16[4,16,8,64]{3,1,2,0:T(8,128)(2,1)S(1)}, bf16[4,16,8,64]{3,1,2,0:T(8,128)(2,1)}, u32[]{:S(2)}) copy-start(bf16[4,16,8,64]{3,1,2,0:T(8,128)(2,1)} %slice.96) | copy-start | bytes 196612
  221.0 8.8 %copy-start.11 = (bf16[4,16,8,64]{3,1,2,0:T(8,128)(2,1)S(1)}, bf16[4,16,8,64]{3,1,2,0:T(8,128)(2,1)}, u32[]{:S(2)}) copy-start(bf16[4,16,8,64]{3,1,2,0:T(8,128)(2,1)} %slice.97) | copy-start | bytes 196612
  222.3 7.8 %copy-start.10 = (bf16[4,16,8,64]{3,1,2,0:T(8,128)(2,1)S(1)}, bf16[4,16,8,64]{3,1,2,0:T(8,128)(2,1)}, u32[]{:S(2)}) copy-start(bf16[4,16,8,64]{3,1,2,0:T(8,128)(2,1)} %slice.98) | copy-start | bytes 196612
  223.4 6.9 %copy-start.9 = (bf16[4,16,8,64]{3,1,2,0:T(8,128)(2,1)S(1)}, bf16[4,16,8,64]{3,1,2,0:T(8,128)(2,1)}, u32[]{:S(2)}) copy-start(bf16[4,16,8,64]{3,1,2,0:T(8,128)(2,1)} %slice.99) | copy-start | bytes 196612
  224.6 5.9 %copy-start.8 = (bf16[4,16,8,64]{3,1,2,0:T(8,128)(2,1)S(1)}, bf16[4,16,8,64]{3,1,2,0:T(8,128)(2,1)}, u32[]{:S(2)}) copy-start(bf16[4,16,8,64]{3,1,2,0:T(8,128)(2,1)} %slice.100) | copy-start | bytes 196612
  224.8 5.9 %copy-start.7 = (bf16[4,16,8,64]{3,1,2,0:T(8,128)(2,1)S(1)}, bf16[4,16,8,64]{3,1,2,0:T(8,128)(2,1)}, u32[]{:S(2)}) copy-start(bf16[4,16,8,64]{3,1,2,0:T(8,128)(2,1)} %slice.101) | copy-start | bytes 196612
  225.0 5.9 %copy-start.6 = (bf16[4,16,8,64]{3,1,2,0:T(8,128)(2,1)S(1)}, bf16[4,16,8,64]{3,1,2,0:T(8,128)(2,1)}, u32[]{:S(2)}) copy-start(bf16[4,16,8,64]{3,1,2,0:T(8,128)(2,1)} %slice.102) | copy-start | bytes 196612
  226.2 5.0 %copy-start.5 = (bf16[4,16,8,64]{3,1,2,0:T(8,128)(2,1)S(1)}, bf16[4,16,8,64]{3,1,2,0:T(8,128)(2,1)}, u32[]{:S(2)}) copy-start(bf16[4,16,8,64]{3,1,2,0:T(8,128)(2,1)} %slice.103) | copy-start | bytes 196612
  227.4 4.0 %copy-start.4 = (bf16[4,16,8,64]{3,1,2,0:T(8,128)(2,1)S(1)}, bf16[4,16,8,64]{3,1,2,0:T(8,128)(2,1)}, u32[]{:S(2)}) copy-start(bf16[4,16,8,64]{3,1,2,0:T(8,128)(2,1)} %slice.104) | copy-start | bytes 196612
  233.4 1.3 copy-start.2
  370.2 2.4 copy-start.1
Sparse Core Ops, SparseCore 0:
  234.8 135.3 all-reduce.3
where the time goes:
time: 381 us; the launch traced here: 380 us
  local copies, waits for them, and re-layouts  204 us (54%)
  waiting for transfers between devices  135 us (35%)
  matrix products  16.5 us (4%)
  between operations  15.2 us (4%)
  starting transfers between devices  4.91 us (1%)
  other arithmetic  4.8 us (1%)
    slice x27, local copies, waits for them, and re-layouts, early_grad(): lax.slice(padded, (a, b, c, 0), (a + 2 * zo - 1, b + 2 * yo - 1, c + 2 *...  194 us
    psum x1, waiting for transfers between devices, total_terms(): summed = lax.psum(flat, ('sample', 'space'))  135 us
    dot_general x27, matrix products, early_grad(): lax.dot_general(piece, flat_delta, (((0,), (0,)), ((), ())), preferred_el...  13.3 us
  transfers between devices with their start and end apart: 2, of which 2 were waited for; matrix products, arithmetic and copies ran while one was open for 0% of the time, Pallas kernels for 0%

commit v1 on v0

--- a/solution.py
+++ b/solution.py
@@ -1,9 +1,19 @@
+import functools
 import jax
 import jax.numpy as jnp
 from jax import lax
 from jax.sharding import PartitionSpec as P
+from jax.lax import psum
 
 SLOPE = 0.3
+
+
+def tell_roots(field_in, bus_axis, ax_name):
+    row_out = psum(field_in, axis_name=bus_axis)
+    return psum(row_out, ax_name)
+
+
+_create_orders = functools.partial(tell_roots, bus_axis="space", ax_name="sample")
 
 
 def passed_along(value, axis, by):
@@ -78,7 +88,7 @@
 
 def total_terms(grad):
     flat = grad.reshape(-1)
-    summed = lax.psum(flat, ("sample", "space"))
+    summed = _create_orders(flat)
     return summed.reshape(grad.shape)
 
 

time: 381 us -> 393 us (1.031)
  waiting for transfers between devices: 135 us -> 150 us
  matrix products: 16.5 us -> 9.76 us
  local copies, waits for them, and re-layouts: 204 us -> 208 us
    psum x1 -> x2, waiting for transfers between devices: 135 us -> 149 us  [the longest x1 101 us: tell_roots(): row_out = psum(field_in, axis_name=bus_axis)]
    dot_general x27, matrix products: 13.3 us -> 7.57 us  [early_grad(): lax.dot_general(piece, flat_delta, (((0,), (0,)), ((), ())), preferred_el...]
  transfers between devices with their start and end apart: 2 -> 3, of which waited for: 2 -> 3; matrix products, arithmetic and copies ran while one was open for 0% -> 0% of each run, Pallas kernels for 0% -> 0%
where the time goes in v1:
time: 393 us
  local copies, waits for them, and re-layouts  208 us (53%)
  waiting for transfers between devices  150 us (38%)
  between operations  15.2 us (4%)
  matrix products  9.76 us (2%)
  starting transfers between devices  4.95 us (1%)
  other arithmetic  4.8 us (1%)
    slice x27, local copies, waits for them, and re-layouts, early_grad(): lax.slice(padded, (a, b, c, 0), (a + 2 * zo - 1, b + 2 * yo - 1, c + 2 *...  194 us
    psum x1, waiting for transfers between devices, tell_roots(): row_out = psum(field_in, axis_name=bus_axis)  101 us
    psum x1, waiting for transfers between devices, tell_roots(): return psum(row_out, ax_name)  48.5 us
  transfers between devices with their start and end apart: 3, of which 3 were waited for; matrix products, arithmetic and copies ran while one was open for 0% of the time, Pallas kernels for 0%

profile of v1, /device:TPU:0, one launch (start us, length us, event | category | flops | bytes accessed | tf_op | source)
XLA Modules:
  0.0 393.0 jit_solution(12593855095702489543)
XLA Ops:
  10.9 4.9 %collective-permute-start = (bf16[32,1024]{1,0:T(8,128)(2,1)S(1)}, bf16[32,1024]{1,0:T(8,128)(2,1)S(1)}, u32[]{:S(2)}, u32[]{:S(2)}) collective-permute-start(bf16[32,1024]{1,0:T(8,128)(2,1)S(1)} %squeeze.11), channel_id=1, source_target_pairs={{0,1},{1,2},{2,3},{3,4},{4,5},{5,6},{6,7},{8,9},{9,10},{10,11},{11... | collective-permute-start | bytes 196616 | tf_op jit(solution)/shard_map/ppermute | solution.py:22
  20.2 9.8 %slice.86 = bf16[4,16,8,64]{3,1,2,0:T(8,128)(2,1)} slice(bf16[9,33,17,64]{3,1,2,0:T(8,128)(2,1)S(1)} %fusion.11), slice={[0:7:2], [0:31:2], [0:15:2], [0:64:1]} | slice | bytes 131072 | tf_op jit(solution)/shard_map/slice | solution.py:72
  30.0 9.7 %slice.87 = bf16[4,16,8,64]{3,1,2,0:T(8,128)(2,1)} slice(bf16[9,33,17,64]{3,1,2,0:T(8,128)(2,1)S(1)} %fusion.11), slice={[0:7:2], [0:31:2], [1:16:2], [0:64:1]} | slice | bytes 131072 | tf_op jit(solution)/shard_map/slice | solution.py:72
  39.8 9.7 %slice.88 = bf16[4,16,8,64]{3,1,2,0:T(8,128)(2,1)} slice(bf16[9,33,17,64]{3,1,2,0:T(8,128)(2,1)S(1)} %fusion.11), slice={[0:7:2], [0:31:2], [2:17:2], [0:64:1]} | slice | bytes 131072 | tf_op jit(solution)/shard_map/slice | solution.py:72
  49.5 9.7 %slice.89 = bf16[4,16,8,64]{3,1,2,0:T(8,128)(2,1)} slice(bf16[9,33,17,64]{3,1,2,0:T(8,128)(2,1)S(1)} %fusion.11), slice={[0:7:2], [1:32:2], [0:15:2], [0:64:1]} | slice | bytes 131072 | tf_op jit(solution)/shard_map/slice | solution.py:72
  59.2 9.7 %slice.90 = bf16[4,16,8,64]{3,1,2,0:T(8,128)(2,1)} slice(bf16[9,33,17,64]{3,1,2,0:T(8,128)(2,1)S(1)} %fusion.11), slice={[0:7:2], [1:32:2], [1:16:2], [0:64:1]} | slice | bytes 131072 | tf_op jit(solution)/shard_map/slice | solution.py:72
  68.9 9.8 %slice.91 = bf16[4,16,8,64]{3,1,2,0:T(8,128)(2,1)} slice(bf16[9,33,17,64]{3,1,2,0:T(8,128)(2,1)S(1)} %fusion.11), slice={[0:7:2], [1:32:2], [2:17:2], [0:64:1]} | slice | bytes 131072 | tf_op jit(solution)/shard_map/slice | solution.py:72
  78.7 9.8 %slice.92 = bf16[4,16,8,64]{3,1,2,0:T(8,128)(2,1)} slice(bf16[9,33,17,64]{3,1,2,0:T(8,128)(2,1)S(1)} %fusion.11), slice={[0:7:2], [2:33:2], [0:15:2], [0:64:1]} | slice | bytes 131072 | tf_op jit(solution)/shard_map/slice | solution.py:72
  88.5 9.8 %slice.93 = bf16[4,16,8,64]{3,1,2,0:T(8,128)(2,1)} slice(bf16[9,33,17,64]{3,1,2,0:T(8,128)(2,1)S(1)} %fusion.11), slice={[0:7:2], [2:33:2], [1:16:2], [0:64:1]} | slice | bytes 131072 | tf_op jit(solution)/shard_map/slice | solution.py:72
  98.2 9.8 %slice.94 = bf16[4,16,8,64]{3,1,2,0:T(8,128)(2,1)} slice(bf16[9,33,17,64]{3,1,2,0:T(8,128)(2,1)S(1)} %fusion.11), slice={[0:7:2], [2:33:2], [2:17:2], [0:64:1]} | slice | bytes 131072 | tf_op jit(solution)/shard_map/slice | solution.py:72
  108.0 9.7 %slice.95 = bf16[4,16,8,64]{3,1,2,0:T(8,128)(2,1)} slice(bf16[9,33,17,64]{3,1,2,0:T(8,128)(2,1)S(1)} %fusion.11), slice={[1:8:2], [0:31:2], [0:15:2], [0:64:1]} | slice | bytes 131072 | tf_op jit(solution)/shard_map/slice | solution.py:72
  117.8 9.7 %slice.96 = bf16[4,16,8,64]{3,1,2,0:T(8,128)(2,1)} slice(bf16[9,33,17,64]{3,1,2,0:T(8,128)(2,1)S(1)} %fusion.11), slice={[1:8:2], [0:31:2], [1:16:2], [0:64:1]} | slice | bytes 131072 | tf_op jit(solution)/shard_map/slice | solution.py:72
  127.5 9.8 %slice.97 = bf16[4,16,8,64]{3,1,2,0:T(8,128)(2,1)} slice(bf16[9,33,17,64]{3,1,2,0:T(8,128)(2,1)S(1)} %fusion.11), slice={[1:8:2], [0:31:2], [2:17:2], [0:64:1]} | slice | bytes 131072 | tf_op jit(solution)/shard_map/slice | solution.py:72
  137.2 9.7 %slice.98 = bf16[4,16,8,64]{3,1,2,0:T(8,128)(2,1)} slice(bf16[9,33,17,64]{3,1,2,0:T(8,128)(2,1)S(1)} %fusion.11), slice={[1:8:2], [1:32:2], [0:15:2], [0:64:1]} | slice | bytes 131072 | tf_op jit(solution)/shard_map/slice | solution.py:72
  147.0 9.7 %slice.99 = bf16[4,16,8,64]{3,1,2,0:T(8,128)(2,1)} slice(bf16[9,33,17,64]{3,1,2,0:T(8,128)(2,1)S(1)} %fusion.11), slice={[1:8:2], [1:32:2], [1:16:2], [0:64:1]} | slice | bytes 131072 | tf_op jit(solution)/shard_map/slice | solution.py:72
  156.7 9.8 %slice.100 = bf16[4,16,8,64]{3,1,2,0:T(8,128)(2,1)} slice(bf16[9,33,17,64]{3,1,2,0:T(8,128)(2,1)S(1)} %fusion.11), slice={[1:8:2], [1:32:2], [2:17:2], [0:64:1]} | slice | bytes 131072 | tf_op jit(solution)/shard_map/slice | solution.py:72
  166.4 9.7 %slice.101 = bf16[4,16,8,64]{3,1,2,0:T(8,128)(2,1)} slice(bf16[9,33,17,64]{3,1,2,0:T(8,128)(2,1)S(1)} %fusion.11), slice={[1:8:2], [2:33:2], [0:15:2], [0:64:1]} | slice | bytes 131072 | tf_op jit(solution)/shard_map/slice | solution.py:72
  176.2 9.7 %slice.102 = bf16[4,16,8,64]{3,1,2,0:T(8,128)(2,1)} slice(bf16[9,33,17,64]{3,1,2,0:T(8,128)(2,1)S(1)} %fusion.11), slice={[1:8:2], [2:33:2], [1:16:2], [0:64:1]} | slice | bytes 131072 | tf_op jit(solution)/shard_map/slice | solution.py:72
  185.9 9.8 %slice.103 = bf16[4,16,8,64]{3,1,2,0:T(8,128)(2,1)} slice(bf16[9,33,17,64]{3,1,2,0:T(8,128)(2,1)S(1)} %fusion.11), slice={[1:8:2], [2:33:2], [2:17:2], [0:64:1]} | slice | bytes 131072 | tf_op jit(solution)/shard_map/slice | solution.py:72
  195.7 9.7 %slice.104 = bf16[4,16,8,64]{3,1,2,0:T(8,128)(2,1)} slice(bf16[9,33,17,64]{3,1,2,0:T(8,128)(2,1)S(1)} %fusion.11), slice={[2:9:2], [0:31:2], [0:15:2], [0:64:1]} | slice | bytes 131072 | tf_op jit(solution)/shard_map/slice | solution.py:72
  230.4 100.6 %all-reduce.6.cloned.1.call-done = (f32[262144]{0:T(1024)}, f32[221184]{0:T(1024)}) async-done(((f32[262144]{0:T(1024)}, f32[221184]{0:T(1024)}), (f32[262144]{0:T(1024)}, f32[221184]{0:T(1024)})) %all-reduce.6.cloned.1.call-update) | async-done | bytes 1933328 | tf_op jit(solution)/shard_map/psum | solution.py:12
  331.0 2.5 reshape.87
  334.4 48.5 %all-reduce.8.cloned.1.call-done = (f32[2,2,2,128,256]{4,3,2,1,0:T(8,128)}, f32[3,3,3,64,128]{4,3,2,1,0:T(8,128)}) async-done(((f32[2,2,2,128,256]{4,3,2,1,0:T(8,128)}, f32[3,3,3,64,128]{4,3,2,1,0:T(8,128)}), (f32[2,2,2,128,256]{4,3,2,1,0:T(8,128)}, f32[3,3,3,64,128]{4,3,2,1,0:T(8,128)})) %all-reduce.8.cloned.1.call-update) | async-done | bytes 1933328 | tf_op jit(solution)/shard_map/psum | solution.py:13
  382.9 2.3 copy.93
  (122 shorter events, 33.8 us)
Async XLA Ops:
  7.2 9.4 %copy-start = (bf16[2,2,2,128,256]{4,3,2,1,0:T(8,128)(2,1)S(1)}, bf16[2,2,2,128,256]{4,3,2,1,0:T(8,128)(2,1)}, u32[]{:S(2)}) copy-start(bf16[2,2,2,128,256]{4,3,2,1,0:T(8,128)(2,1)} %param.12) | copy-start | bytes 1572868
  7.2 9.3 %copy-start.3 = (bf16[1,2,8,1024]{3,2,1,0:T(8,128)(2,1)S(1)}, bf16[1,2,8,1024]{3,2,1,0:T(8,128)(2,1)}, u32[]{:S(2)}) copy-start(bf16[1,2,8,1024]{3,2,1,0:T(8,128)(2,1)} %param.13) | copy-start | bytes 98308
  7.2 323.8 %all-reduce.6.cloned.1.call-start = ((), (), s32[]{:S(2)}) async-start(), calls=%async_computation | async-start | bytes 3866624 | tf_op jit(solution)/shard_map/psum | solution.py:12
  9.0 7.9 %copy-start.22 = (f32[8,128]{1,0:T(8,128)S(1)}, f32[8,128]{1,0:T(8,128)}, u32[]{:S(2)}) copy-start(f32[8,128]{1,0:T(8,128)} %param.11) | copy-start | bytes 12292
  10.9 6.8 %collective-permute-start = (bf16[32,1024]{1,0:T(8,128)(2,1)S(1)}, bf16[32,1024]{1,0:T(8,128)(2,1)S(1)}, u32[]{:S(2)}, u32[]{:S(2)}) collective-permute-start(bf16[32,1024]{1,0:T(8,128)(2,1)S(1)} %squeeze.11), channel_id=1, source_target_pairs={{0,1},{1,2},{2,3},{3,4},{4,5},{5,6},{6,7},{8,9},{9,10},{10,11},{11... | collective-permute-start | bytes 196616 | tf_op jit(solution)/shard_map/ppermute | solution.py:22
  219.4 4.5 %copy-start.20 = (bf16[4,16,8,64]{3,1,2,0:T(8,128)(2,1)S(1)}, bf16[4,16,8,64]{3,1,2,0:T(8,128)(2,1)}, u32[]{:S(2)}) copy-start(bf16[4,16,8,64]{3,1,2,0:T(8,128)(2,1)} %slice.88) | copy-start | bytes 196612
  219.7 4.4 %copy-start.19 = (bf16[4,16,8,64]{3,1,2,0:T(8,128)(2,1)S(1)}, bf16[4,16,8,64]{3,1,2,0:T(8,128)(2,1)}, u32[]{:S(2)}) copy-start(bf16[4,16,8,64]{3,1,2,0:T(8,128)(2,1)} %slice.89) | copy-start | bytes 196612
  219.7 4.7 %copy-start.18 = (bf16[4,16,8,64]{3,1,2,0:T(8,128)(2,1)S(1)}, bf16[4,16,8,64]{3,1,2,0:T(8,128)(2,1)}, u32[]{:S(2)}) copy-start(bf16[4,16,8,64]{3,1,2,0:T(8,128)(2,1)} %slice.90) | copy-start | bytes 196612
  220.1 4.6 %copy-start.17 = (bf16[4,16,8,64]{3,1,2,0:T(8,128)(2,1)S(1)}, bf16[4,16,8,64]{3,1,2,0:T(8,128)(2,1)}, u32[]{:S(2)}) copy-start(bf16[4,16,8,64]{3,1,2,0:T(8,128)(2,1)} %slice.91) | copy-start | bytes 196612
  220.1 4.8 %copy-start.16 = (bf16[4,16,8,64]{3,1,2,0:T(8,128)(2,1)S(1)}, bf16[4,16,8,64]{3,1,2,0:T(8,128)(2,1)}, u32[]{:S(2)}) copy-start(bf16[4,16,8,64]{3,1,2,0:T(8,128)(2,1)} %slice.92) | copy-start | bytes 196612
  220.1 5.0 %copy-start.15 = (bf16[4,16,8,64]{3,1,2,0:T(8,128)(2,1)S(1)}, bf16[4,16,8,64]{3,1,2,0:T(8,128)(2,1)}, u32[]{:S(2)}) copy-start(bf16[4,16,8,64]{3,1,2,0:T(8,128)(2,1)} %slice.93) | copy-start | bytes 196612
  221.6 3.7 copy-start.14
  221.6 3.9 copy-start.13
  221.6 4.1 %copy-start.12 = (bf16[4,16,8,64]{3,1,2,0:T(8,128)(2,1)S(1)}, bf16[4,16,8,64]{3,1,2,0:T(8,128)(2,1)}, u32[]{:S(2)}) copy-start(bf16[4,16,8,64]{3,1,2,0:T(8,128)(2,1)} %slice.96) | copy-start | bytes 196612
  222.8 3.2 copy-start.11
  224.0 2.3 copy-start.10
  224.2 2.2 copy-start.9
  224.4 2.2 copy-start.8
  224.6 2.2 copy-start.7
  224.9 2.2 copy-start.6
  225.1 2.2 copy-start.5
  225.3 2.2 copy-start.4
  230.4 152.5 %all-reduce.8.cloned.1.call-start = ((), (), s32[]{:S(2)}) async-start(), calls=%async_computation.1 | async-start | bytes 3866624 | tf_op jit(solution)/shard_map/psum | solution.py:13
  382.9 2.4 copy-start.1
  (4 other events, 4.8 us)
Sparse Core Ops, SparseCore 0:
  230.5 100.4 all-reduce.5
  334.2 48.5 all-reduce.7
